TPU v7x, 512 devices: a whole 4x8x8 slice. The times are simulated.
512 devices in a mesh: gx: 32 (over x_lo, z, core), gy: 16 (over y, x_hi).
Axes of the slice: x: 4 (x_hi: 2, x_lo: 2; x = x_hi * 2 + x_lo), y: 8, z: 8, core: 2. Of those that a mesh axis runs over, the one named last changes fastest.
Arguments:
- currents: bfloat16 [1024, 512, 2, 128], P('gx', 'gy'), may hold values from -6 to 6
- box_count: int32 [1024, 512], P('gx', 'gy'), may hold values from 0 to 128, as said below
- aggregate: bfloat16 [256, 256], replicated, may hold values from -0.375 to 0.375
- near_blocks: bfloat16 [9, 256, 256], replicated, may hold values from -0.125 to 0.125
- low_translator: float32 [16, 2, 128], replicated, may hold values from -1.5 to 1.5
- child_to_parent: bfloat16 [4, 256, 512], replicated, may hold values from -0.1875 to 0.1875
- coarse_list: int32 [512, 256, 16], P('gx', 'gy'), may hold values from 0 to 4095
- coarse_kind: int32 [512, 256, 16], P('gx', 'gy'), may hold values from 0 to 63
- coarse_count: int32 [512, 256], P('gx', 'gy'), may hold values from 1 to 16, as said below
- up_translator: float32 [64, 2, 256], replicated, may hold values from -1.5 to 1.5
- parent_to_child: bfloat16 [4, 512, 256], replicated, may hold values from -0.25 to 0.25
- receive_map: bfloat16 [256, 256], replicated, may hold values from -0.375 to 0.375
Outputs:
- field: float32 [1024, 512, 2, 128], P('gx', 'gy')
Inputs may be any that keep to these rules, and one draw needn't show every extreme that they name: `box_count`: ground clutter makes some boxes full and most sparse; some box holds 128 unknowns and some none. `coarse_count`: some list uses all 16 entries.
All inputs are finite; a program needn't handle non-finite values.
Results may differ from a plain program's by a relative error of at most 0.0041.
Values may be sent and summed in bfloat16 or wider, within the bound.
A program may use at most 128 MiB of HBM per device.

v0:
```python
import jax
import jax.numpy as jnp
from jax import lax
from jax.sharding import PartitionSpec as P


def extended(cells, sides, width):
    for axis, dim in sides:
        count = lax.axis_size(axis)
        ends = count - 1
        head = lax.slice_in_dim(cells, 0, width, axis=dim)
        tail = lax.slice_in_dim(cells, cells.shape[dim] - width, cells.shape[dim], axis=dim)
        cells = jnp.concatenate(
            [
                lax.ppermute(tail, axis, [(i, (i + 1) % count) for i in range(ends)]),
                cells,
                lax.ppermute(head, axis, [((i + 1) % count, i) for i in range(ends)]),
            ],
            axis=dim,
        )
    return cells


def complex_flat(table, pattern, half):
    real_part = pattern[..., :half].astype(jnp.float32)
    imag_part = pattern[..., half:].astype(jnp.float32)
    first = table[..., :half] * real_part - table[..., half:] * imag_part
    second = table[..., :half] * imag_part + table[..., half:] * real_part
    return jnp.concatenate([first, second], axis=-1)


def make_patterns(block, aggregate):
    size_a, size_b = (block.shape[0], block.shape[1])
    flat_block = block.reshape(size_a * size_b, block.shape[2] * block.shape[3])
    result = jnp.dot(flat_block, aggregate, preferred_element_type=jnp.float32)
    return result.astype(jnp.bfloat16).reshape(size_a, size_b, aggregate.shape[1])


def translate_group(flat_group, lists, kinds, counts, table):
    rows_a, rows_b, slots = lists.shape
    kind_total, width_two = table.shape
    half = width_two // 2
    kind_ids = jnp.arange(kind_total, dtype=jnp.int32)[None, :]

    def accumulate(slot, total):
        index = lists[:, :, slot].reshape(rows_a * rows_b)
        source = jnp.take(flat_group, index, axis=0)
        choose = (kinds[:, :, slot].reshape(rows_a * rows_b)[:, None] == kind_ids).astype(
            jnp.float32
        )
        factors = jnp.dot(
            choose, table, precision=lax.Precision.HIGHEST, preferred_element_type=jnp.float32
        )
        term = complex_flat(factors, source, half)
        keep = (slot < counts).reshape(rows_a * rows_b)
        return total + jnp.where(keep[:, None], term, jnp.zeros_like(term))

    start = jnp.zeros((rows_a * rows_b, width_two), jnp.float32)
    result = lax.fori_loop(0, slots, accumulate, start)
    return result.astype(jnp.bfloat16).reshape(rows_a, rows_b, width_two)


def body(
    currents,
    box_count,
    aggregate,
    near_blocks,
    low_translator,
    child_to_parent,
    coarse_list,
    coarse_kind,
    coarse_count,
    up_translator,
    parent_to_child,
    receive_map,
):
    tile_x, tile_y = box_count.shape
    unknowns = currents.shape[-1]
    samples = low_translator.shape[-1]
    parent_samples = up_translator.shape[-1]
    kind_total = up_translator.shape[0]
    low_flat = low_translator.reshape(low_translator.shape[0], 2 * samples)
    mask = jnp.arange(unknowns, dtype=jnp.int32)[None, None, :] < box_count[:, :, None]
    live = jnp.where(mask[:, :, None, :], currents, jnp.zeros_like(currents))
    near_pad = extended(live, (("gx", 0), ("gy", 1)), 1)
    pattern = make_patterns(live, aggregate)
    pattern_pad = extended(pattern, (("gx", 0), ("gy", 1)), 2)
    lower_in = jnp.zeros((tile_x, tile_y, 2 * samples), jnp.float32)
    offset = 0
    for shift_x in range(-2, 3):
        for shift_y in range(-2, 3):
            if max(abs(shift_x), abs(shift_y)) < 2:
                continue
            source = pattern_pad[
                2 + shift_x : 2 + shift_x + tile_x, 2 + shift_y : 2 + shift_y + tile_y
            ]
            lower_in = lower_in + complex_flat(low_flat[offset], source, samples)
            offset += 1
    parents_x, parents_y = (tile_x // 2, tile_y // 2)
    children = pattern.reshape(parents_x, 2, parents_y, 2, 2 * samples)
    coarse_sum = jnp.zeros((parents_x * parents_y, 2 * parent_samples), jnp.float32)
    for half_x in range(2):
        for half_y in range(2):
            child = children[:, half_x, :, half_y].reshape(parents_x * parents_y, 2 * samples)
            coarse_sum = coarse_sum + jnp.dot(
                child, child_to_parent[2 * half_x + half_y], preferred_element_type=jnp.float32
            )
    coarse = coarse_sum.astype(jnp.bfloat16).reshape(parents_x, parents_y, 2 * parent_samples)
    group = lax.all_gather(coarse, "gy", axis=1, tiled=True)
    flat_group = group.reshape(group.shape[0] * group.shape[1], 2 * parent_samples)
    table = up_translator.reshape(kind_total, 2 * parent_samples)
    coarse_in = translate_group(flat_group, coarse_list, coarse_kind, coarse_count, table)
    coarse_flat = coarse_in.reshape(parents_x * parents_y, 2 * parent_samples)
    pieces = [
        jnp.dot(coarse_flat, parent_to_child[child_id], preferred_element_type=jnp.float32).reshape(
            parents_x, parents_y, 2 * samples
        )
        for child_id in range(4)
    ]
    rows_first = jnp.stack([pieces[0], pieces[1]], axis=2)
    rows_second = jnp.stack([pieces[2], pieces[3]], axis=2)
    from_parent = jnp.stack([rows_first, rows_second], axis=1).reshape(tile_x, tile_y, 2 * samples)
    incoming = (lower_in + from_parent).astype(jnp.bfloat16)
    field = jnp.dot(
        incoming.reshape(tile_x * tile_y, 2 * samples),
        receive_map,
        preferred_element_type=jnp.float32,
    )
    for shift_x in range(-1, 2):
        for shift_y in range(-1, 2):
            source = near_pad[
                1 + shift_x : 1 + shift_x + tile_x, 1 + shift_y : 1 + shift_y + tile_y
            ].reshape(tile_x * tile_y, 2 * unknowns)
            field = field + jnp.dot(
                source,
                near_blocks[3 * (shift_x + 1) + shift_y + 1],
                preferred_element_type=jnp.float32,
            )
    return field.reshape(tile_x, tile_y, 2, unknowns) * mask[:, :, None, :].astype(jnp.float32)


def solution(mesh):
    in_specs = (
        P("gx", "gy", None, None),
        P("gx", "gy"),
        P(),
        P(),
        P(),
        P(),
        P("gx", "gy", None),
        P("gx", "gy", None),
        P("gx", "gy"),
        P(),
        P(),
        P(),
    )
    out_specs = P("gx", "gy", None, None)
    return jax.shard_map(body, mesh=mesh, in_specs=in_specs, out_specs=out_specs, check_vma=False)
```

profile of v0, /device:TPU:8, one launch (start us, length us, event | category | flops | bytes accessed | tf_op | source)
XLA Modules:
  0.0 233.4 jit_solution(2320973562088822764)
XLA Ops:
  17.9 5.2 %collective-permute-start.4 = (bf16[1,32,2,128]{3,2,1,0:T(2,128)(2,1)S(1)}, bf16[1,32,2,128]{3,2,1,0:T(2,128)(2,1)S(1)}, u32[]{:S(2)}, u32[]{:S(2)}) collective-permute-start(bf16[1,32,2,128]{3,2,1,0:T(2,128)(2,1)S(1)} %get-tuple-element.260), channel_id=1, source_target_pairs={{0,16},{16,32},{32,48},{48,64},{64,80},{80,96},{96,112},{112,128},... | collective-permute-start | bytes 49160 | tf_op jit(solution)/shard_map/ppermute | solution.py:15
  27.5 4.9 %collective-permute-start.6 = (bf16[34,1,2,128]{3,2,1,0:T(2,128)(2,1)S(1)}, bf16[34,1,2,128]{3,2,1,0:T(2,128)(2,1)S(1)}, u32[]{:S(2)}, u32[]{:S(2)}) collective-permute-start(bf16[34,1,2,128]{3,2,1,0:T(2,128)(2,1)S(1)} %get-tuple-element.257), channel_id=1, source_target_pairs={{0,1},{1,2},{2,3},{3,4},{4,5},{5,6},{6,7},{7,8},{8,9},{9,10},{10,1... | collective-permute-start | bytes 52232 | tf_op jit(solution)/shard_map/ppermute | solution.py:15
  38.2 4.0 %collective-permute-start.2 = (bf16[36,2,256]{2,1,0:T(2,128)(2,1)S(1)}, bf16[36,2,256]{2,1,0:T(2,128)(2,1)S(1)}, u32[]{:S(2)}, u32[]{:S(2)}) collective-permute-start(bf16[36,2,256]{2,1,0:T(2,128)(2,1)S(1)} %get-tuple-element.242), channel_id=1, source_target_pairs={{0,1},{1,2},{2,3},{3,4},{4,5},{5,6},{6,7},{7,8},{8,9},{9,10},{10,1... | collective-permute-start | bytes 110600 | tf_op jit(solution)/shard_map/ppermute | solution.py:15
  42.3 4.4 %collective-permute-start.3 = (bf16[36,2,256]{2,1,0:T(2,128)(2,1)S(1)}, bf16[36,2,256]{2,1,0:T(2,128)(2,1)S(1)}, u32[]{:S(2)}, u32[]{:S(2)}) collective-permute-start(bf16[36,2,256]{2,1,0:T(2,128)(2,1)S(1)} %get-tuple-element.243), channel_id=1, source_target_pairs={{1,0},{2,1},{3,2},{4,3},{5,4},{6,5},{7,6},{8,7},{9,8},{10,9},{11,1... | collective-permute-start | bytes 110600 | tf_op jit(solution)/shard_map/ppermute | solution.py:17
  51.1 4.4 %fusion.115 = (bf16[32,32,2,128]{3,2,1,0:T(2,128)(2,1)}, bf16[32,32,2,128]{3,2,1,0:T(2,128)(2,1)}, bf16[32,32,2,128]{3,2,1,0:T(2,128)(2,1)}, bf16[32,32,2,128]{3...) fusion(bf16[34,33,2,128]{3,2,1,0:T(2,128)(2,1)S(1)} %get-tuple-element.254, ...), kind=kLoop, calls=%fused_computation.264 | loop fusion | bytes 6291456 | tf_op jit(solution)/shard_map/slice | solution.py:131
  66.8 58.1 %all-gather.2.cloned.1.call-done = bf16[16,256,512]{2,1,0:T(8,128)(2,1)} async-done(((bf16[16,16,512]{2,1,0:T(8,128)(2,1)}), bf16[16,256,512]{2,1,0:T(8,128)(2,1)}) %all-gather.2.cloned.1.call-update) | async-done | bytes 4194320 | tf_op jit(solution)/shard_map/all_gather | solution.py:109
  125.0 81.5 %while.14 = (s32[]{:T(128)}, f32[256,512]{1,0:T(8,128)S(1)}, s32[16,16]{1,0:T(8,128)S(1)}, s32[16,16,16]{1,0,2:T(8,128)S(1)}, f32[64,512]{1,0:T(8,128)S(1)}, /*i...) while((s32[]{:T(128)}, f32[256,512]{1,0:T(8,128)S(1)}, ...), condition=%wide.region_1.2_spmd.clone, body=%wide.region_0.1_spmd.clone.sunk | while | flops 101862912 | bytes 4610671 | solution.py:59
  125.1 4.0 %gather_fusion = bf16[256,512]{1,0:T(8,128)(2,1)S(1)} fusion(bf16[4096,512]{1,0:T(8,128)(2,1)} %get-tuple-element.384, s32[1024]{0:T(1024)S(1)} %pad_clamp_fusion.2), kind=kCustom, calls=%fused_computation.clone.clone.1 | custom fusion | bytes 525312 | tf_op jit(solution)/shard_map/while/body/eval_jaxpr/jit(_take)/gather | solution.py:47
  130.2 3.9 %gather_fusion = bf16[256,512]{1,0:T(8,128)(2,1)S(1)} fusion(bf16[4096,512]{1,0:T(8,128)(2,1)} %get-tuple-element.384, s32[1024]{0:T(1024)S(1)} %pad_clamp_fusion.2), kind=kCustom, calls=%fused_computation.clone.clone.1 | custom fusion | bytes 525312 | tf_op jit(solution)/shard_map/while/body/eval_jaxpr/jit(_take)/gather | solution.py:47
  135.3 3.9 %gather_fusion = bf16[256,512]{1,0:T(8,128)(2,1)S(1)} fusion(bf16[4096,512]{1,0:T(8,128)(2,1)} %get-tuple-element.384, s32[1024]{0:T(1024)S(1)} %pad_clamp_fusion.2), kind=kCustom, calls=%fused_computation.clone.clone.1 | custom fusion | bytes 525312 | tf_op jit(solution)/shard_map/while/body/eval_jaxpr/jit(_take)/gather | solution.py:47
  140.4 3.9 %gather_fusion = bf16[256,512]{1,0:T(8,128)(2,1)S(1)} fusion(bf16[4096,512]{1,0:T(8,128)(2,1)} %get-tuple-element.384, s32[1024]{0:T(1024)S(1)} %pad_clamp_fusion.2), kind=kCustom, calls=%fused_computation.clone.clone.1 | custom fusion | bytes 525312 | tf_op jit(solution)/shard_map/while/body/eval_jaxpr/jit(_take)/gather | solution.py:47
  145.5 3.9 %gather_fusion = bf16[256,512]{1,0:T(8,128)(2,1)S(1)} fusion(bf16[4096,512]{1,0:T(8,128)(2,1)} %get-tuple-element.384, s32[1024]{0:T(1024)S(1)} %pad_clamp_fusion.2), kind=kCustom, calls=%fused_computation.clone.clone.1 | custom fusion | bytes 525312 | tf_op jit(solution)/shard_map/while/body/eval_jaxpr/jit(_take)/gather | solution.py:47
  150.6 3.9 %gather_fusion = bf16[256,512]{1,0:T(8,128)(2,1)S(1)} fusion(bf16[4096,512]{1,0:T(8,128)(2,1)} %get-tuple-element.384, s32[1024]{0:T(1024)S(1)} %pad_clamp_fusion.2), kind=kCustom, calls=%fused_computation.clone.clone.1 | custom fusion | bytes 525312 | tf_op jit(solution)/shard_map/while/body/eval_jaxpr/jit(_take)/gather | solution.py:47
  155.7 3.9 %gather_fusion = bf16[256,512]{1,0:T(8,128)(2,1)S(1)} fusion(bf16[4096,512]{1,0:T(8,128)(2,1)} %get-tuple-element.384, s32[1024]{0:T(1024)S(1)} %pad_clamp_fusion.2), kind=kCustom, calls=%fused_computation.clone.clone.1 | custom fusion | bytes 525312 | tf_op jit(solution)/shard_map/while/body/eval_jaxpr/jit(_take)/gather | solution.py:47
  160.8 3.9 %gather_fusion = bf16[256,512]{1,0:T(8,128)(2,1)S(1)} fusion(bf16[4096,512]{1,0:T(8,128)(2,1)} %get-tuple-element.384, s32[1024]{0:T(1024)S(1)} %pad_clamp_fusion.2), kind=kCustom, calls=%fused_computation.clone.clone.1 | custom fusion | bytes 525312 | tf_op jit(solution)/shard_map/while/body/eval_jaxpr/jit(_take)/gather | solution.py:47
  165.9 3.9 %gather_fusion = bf16[256,512]{1,0:T(8,128)(2,1)S(1)} fusion(bf16[4096,512]{1,0:T(8,128)(2,1)} %get-tuple-element.384, s32[1024]{0:T(1024)S(1)} %pad_clamp_fusion.2), kind=kCustom, calls=%fused_computation.clone.clone.1 | custom fusion | bytes 525312 | tf_op jit(solution)/shard_map/while/body/eval_jaxpr/jit(_take)/gather | solution.py:47
  171.0 3.9 %gather_fusion = bf16[256,512]{1,0:T(8,128)(2,1)S(1)} fusion(bf16[4096,512]{1,0:T(8,128)(2,1)} %get-tuple-element.384, s32[1024]{0:T(1024)S(1)} %pad_clamp_fusion.2), kind=kCustom, calls=%fused_computation.clone.clone.1 | custom fusion | bytes 525312 | tf_op jit(solution)/shard_map/while/body/eval_jaxpr/jit(_take)/gather | solution.py:47
  176.1 3.9 %gather_fusion = bf16[256,512]{1,0:T(8,128)(2,1)S(1)} fusion(bf16[4096,512]{1,0:T(8,128)(2,1)} %get-tuple-element.384, s32[1024]{0:T(1024)S(1)} %pad_clamp_fusion.2), kind=kCustom, calls=%fused_computation.clone.clone.1 | custom fusion | bytes 525312 | tf_op jit(solution)/shard_map/while/body/eval_jaxpr/jit(_take)/gather | solution.py:47
  181.1 3.9 %gather_fusion = bf16[256,512]{1,0:T(8,128)(2,1)S(1)} fusion(bf16[4096,512]{1,0:T(8,128)(2,1)} %get-tuple-element.384, s32[1024]{0:T(1024)S(1)} %pad_clamp_fusion.2), kind=kCustom, calls=%fused_computation.clone.clone.1 | custom fusion | bytes 525312 | tf_op jit(solution)/shard_map/while/body/eval_jaxpr/jit(_take)/gather | solution.py:47
  186.2 3.9 %gather_fusion = bf16[256,512]{1,0:T(8,128)(2,1)S(1)} fusion(bf16[4096,512]{1,0:T(8,128)(2,1)} %get-tuple-element.384, s32[1024]{0:T(1024)S(1)} %pad_clamp_fusion.2), kind=kCustom, calls=%fused_computation.clone.clone.1 | custom fusion | bytes 525312 | tf_op jit(solution)/shard_map/while/body/eval_jaxpr/jit(_take)/gather | solution.py:47
  191.3 3.9 %gather_fusion = bf16[256,512]{1,0:T(8,128)(2,1)S(1)} fusion(bf16[4096,512]{1,0:T(8,128)(2,1)} %get-tuple-element.384, s32[1024]{0:T(1024)S(1)} %pad_clamp_fusion.2), kind=kCustom, calls=%fused_computation.clone.clone.1 | custom fusion | bytes 525312 | tf_op jit(solution)/shard_map/while/body/eval_jaxpr/jit(_take)/gather | solution.py:47
  196.4 3.9 %gather_fusion = bf16[256,512]{1,0:T(8,128)(2,1)S(1)} fusion(bf16[4096,512]{1,0:T(8,128)(2,1)} %get-tuple-element.384, s32[1024]{0:T(1024)S(1)} %pad_clamp_fusion.2), kind=kCustom, calls=%fused_computation.clone.clone.1 | custom fusion | bytes 525312 | tf_op jit(solution)/shard_map/while/body/eval_jaxpr/jit(_take)/gather | solution.py:47
  201.5 3.9 %gather_fusion = bf16[256,512]{1,0:T(8,128)(2,1)S(1)} fusion(bf16[4096,512]{1,0:T(8,128)(2,1)} %get-tuple-element.384, s32[1024]{0:T(1024)S(1)} %pad_clamp_fusion.2), kind=kCustom, calls=%fused_computation.clone.clone.1 | custom fusion | bytes 525312 | tf_op jit(solution)/shard_map/while/body/eval_jaxpr/jit(_take)/gather | solution.py:47
  209.5 6.5 %fusion.74 = f32[1024,256]{1,0:T(8,128)S(1)} fusion(bf16[256,256]{1,0:T(8,128)(2,1)S(1)} %copy-done.15, f32[1024,256]{1,0:T(8,128)S(1)} %reshape.262, f32[1024,128]{1,0:T(8,128)} %bitcast.276, f32[1024,128]{1,0:T(8,128)} %bitcast.277, f32[1024,128]{1,0:T(8,128)} %bitcast.278, f32[1024,128]{1,0:T(8,128)} %bitcast.279, f32[1024,128]{1,0:T(8,128)} %bitcast.289, ...), kind=kOutput, calls=%fused_computation.182 | convolution fusion | flops 142868480 | bytes 19005440 | tf_op jit(solution)/shard_map/dot_general | solution.py:124
  (315 shorter events, 67.8 us)
Async XLA Ops:
  6.5 3.7 %copy-start = (bf16[256,256]{1,0:T(8,128)(2,1)S(1)}, bf16[256,256]{1,0:T(8,128)(2,1)}, u32[]{:S(2)}) copy-start(bf16[256,256]{1,0:T(8,128)(2,1)} %param.16) | copy-start | bytes 393220
  6.5 118.4 %all-gather.2.cloned.1.call-start = ((), (), s32[]{:S(2)}) async-start(), calls=%async_computation | async-start | bytes 4456448 | tf_op jit(solution)/shard_map/all_gather | solution.py:109
  11.9 1.2 copy-start.13
  13.8 10.6 %copy-start.19 = (f32[16,2,128]{2,1,0:T(2,128)S(1)}, f32[16,2,128]{2,1,0:T(2,128)}, u32[]{:S(2)}) copy-start(f32[16,2,128]{2,1,0:T(2,128)} %param.18) | copy-start | bytes 49156
  13.8 10.7 %copy-start.16 = (f32[64,2,256]{2,1,0:T(2,128)S(1)}, f32[64,2,256]{2,1,0:T(2,128)}, u32[]{:S(2)}) copy-start(f32[64,2,256]{2,1,0:T(2,128)} %param.23) | copy-start | bytes 393220
  13.8 10.7 %copy-start.17 = (s32[16,16,16]{2,1,0:T(8,128)S(1)}, s32[16,16,16]{2,1,0:T(8,128)}, u32[]{:S(2)}) copy-start(s32[16,16,16]{2,1,0:T(8,128)} %param.21) | copy-start | bytes 49156
  13.8 10.8 %copy-start.18 = (s32[16,16,16]{2,1,0:T(8,128)S(1)}, s32[16,16,16]{2,1,0:T(8,128)}, u32[]{:S(2)}) copy-start(s32[16,16,16]{2,1,0:T(8,128)} %param.20) | copy-start | bytes 49156
  14.8 23.3 %collective-permute-start = (bf16[2,32,256]{2,1,0:T(8,128)(2,1)S(1)}, bf16[2,32,256]{2,1,0:T(8,128)(2,1)S(1)}, u32[]{:S(2)}, u32[]{:S(2)}) collective-permute-start(bf16[2,32,256]{2,1,0:T(8,128)(2,1)S(1)} %bitcast.304), channel_id=1, source_target_pairs={{0,16},{16,32},{32,48},{48,64},{64,80},{80,96},{96,112},{112,128},... | collective-permute-start | bytes 98312 | tf_op jit(solution)/shard_map/ppermute | solution.py:15
  16.6 21.6 %collective-permute-start.1 = (bf16[2,32,256]{2,1,0:T(8,128)(2,1)S(1)}, bf16[2,32,256]{2,1,0:T(8,128)(2,1)S(1)}, u32[]{:S(2)}, u32[]{:S(2)}) collective-permute-start(bf16[2,32,256]{2,1,0:T(8,128)(2,1)S(1)} %bitcast.303), channel_id=1, source_target_pairs={{16,0},{32,16},{48,32},{64,48},{80,64},{96,80},{112,96},{128,112},... | collective-permute-start | bytes 98312 | tf_op jit(solution)/shard_map/ppermute | solution.py:17
  17.9 6.8 %collective-permute-start.4 = (bf16[1,32,2,128]{3,2,1,0:T(2,128)(2,1)S(1)}, bf16[1,32,2,128]{3,2,1,0:T(2,128)(2,1)S(1)}, u32[]{:S(2)}, u32[]{:S(2)}) collective-permute-start(bf16[1,32,2,128]{3,2,1,0:T(2,128)(2,1)S(1)} %get-tuple-element.260), channel_id=1, source_target_pairs={{0,16},{16,32},{32,48},{48,64},{64,80},{80,96},{96,112},{112,128},... | collective-permute-start | bytes 49160 | tf_op jit(solution)/shard_map/ppermute | solution.py:15
  23.1 4.3 %collective-permute-start.5 = (bf16[1,32,2,128]{3,2,1,0:T(2,128)(2,1)S(1)}, bf16[1,32,2,128]{3,2,1,0:T(2,128)(2,1)S(1)}, u32[]{:S(2)}, u32[]{:S(2)}) collective-permute-start(bf16[1,32,2,128]{3,2,1,0:T(2,128)(2,1)S(1)} %get-tuple-element.261), channel_id=1, source_target_pairs={{16,0},{32,16},{48,32},{64,48},{80,64},{96,80},{112,96},{128,112},... | collective-permute-start | bytes 49160 | tf_op jit(solution)/shard_map/ppermute | solution.py:17
  27.5 21.5 %collective-permute-start.6 = (bf16[34,1,2,128]{3,2,1,0:T(2,128)(2,1)S(1)}, bf16[34,1,2,128]{3,2,1,0:T(2,128)(2,1)S(1)}, u32[]{:S(2)}, u32[]{:S(2)}) collective-permute-start(bf16[34,1,2,128]{3,2,1,0:T(2,128)(2,1)S(1)} %get-tuple-element.257), channel_id=1, source_target_pairs={{0,1},{1,2},{2,3},{3,4},{4,5},{5,6},{6,7},{7,8},{8,9},{9,10},{10,1... | collective-permute-start | bytes 52232 | tf_op jit(solution)/shard_map/ppermute | solution.py:15
  32.4 16.5 %collective-permute-start.7 = (bf16[34,1,2,128]{3,2,1,0:T(2,128)(2,1)S(1)}, bf16[34,1,2,128]{3,2,1,0:T(2,128)(2,1)S(1)}, u32[]{:S(2)}, u32[]{:S(2)}) collective-permute-start(bf16[34,1,2,128]{3,2,1,0:T(2,128)(2,1)S(1)} %get-tuple-element.256), channel_id=1, source_target_pairs={{1,0},{2,1},{3,2},{4,3},{5,4},{6,5},{7,6},{8,7},{9,8},{10,9},{11,1... | collective-permute-start | bytes 52232 | tf_op jit(solution)/shard_map/ppermute | solution.py:17
  38.2 17.3 %collective-permute-start.2 = (bf16[36,2,256]{2,1,0:T(2,128)(2,1)S(1)}, bf16[36,2,256]{2,1,0:T(2,128)(2,1)S(1)}, u32[]{:S(2)}, u32[]{:S(2)}) collective-permute-start(bf16[36,2,256]{2,1,0:T(2,128)(2,1)S(1)} %get-tuple-element.242), channel_id=1, source_target_pairs={{0,1},{1,2},{2,3},{3,4},{4,5},{5,6},{6,7},{7,8},{8,9},{9,10},{10,1... | collective-permute-start | bytes 110600 | tf_op jit(solution)/shard_map/ppermute | solution.py:15
  42.3 13.2 %collective-permute-start.3 = (bf16[36,2,256]{2,1,0:T(2,128)(2,1)S(1)}, bf16[36,2,256]{2,1,0:T(2,128)(2,1)S(1)}, u32[]{:S(2)}, u32[]{:S(2)}) collective-permute-start(bf16[36,2,256]{2,1,0:T(2,128)(2,1)S(1)} %get-tuple-element.243), channel_id=1, source_target_pairs={{1,0},{2,1},{3,2},{4,3},{5,4},{6,5},{7,6},{8,7},{9,8},{10,9},{11,1... | collective-permute-start | bytes 110600 | tf_op jit(solution)/shard_map/ppermute | solution.py:17
  64.4 60.5 %copy-start.14 = (s32[16,16]{1,0:T(8,128)S(1)}, s32[16,16]{1,0:T(8,128)}, u32[]{:S(2)}) copy-start(s32[16,16]{1,0:T(8,128)} %param.22) | copy-start | bytes 3076
  125.0 81.6 %copy-start.12 = (bf16[4,512,256]{2,1,0:T(8,128)(2,1)S(1)}, bf16[4,512,256]{2,1,0:T(8,128)(2,1)}, u32[]{:S(2)}) copy-start(bf16[4,512,256]{2,1,0:T(8,128)(2,1)} %param.24) | copy-start | bytes 3145732
  208.5 1.0 copy-start.1
  208.5 1.1 copy-start.15
  209.5 6.5 %copy-start.10 = (bf16[32,32,2,128]{3,2,1,0:T(2,128)(2,1)S(1)}, bf16[32,32,2,128]{3,2,1,0:T(2,128)(2,1)}, u32[]{:S(2)}) copy-start(bf16[32,32,2,128]{3,2,1,0:T(2,128)(2,1)} %get-tuple-element.302) | copy-start | bytes 1572868
  209.5 6.5 %copy-start.11 = (bf16[9,256,256]{2,1,0:T(8,128)(2,1)S(1)}, bf16[9,256,256]{2,1,0:T(8,128)(2,1)}, u32[]{:S(2)}) copy-start(bf16[9,256,256]{2,1,0:T(8,128)(2,1)} %param.17) | copy-start | bytes 3538948
  216.1 1.0 copy-start.4
  219.5 1.0 copy-start.7
  224.0 1.0 copy-start.2
  (5 other events, 5.2 us)
Sparse Core Ops, SparseCore 0:
  14.9 109.9 all-gather.1
where the time goes:
time: 235 us; the launch traced here: 233 us
  local copies, waits for them, and re-layouts  83.8 us (36%)
  waiting for transfers between devices  60.8 us (26%)
  other arithmetic  29.2 us (12%)
  starting transfers between devices  26.2 us (11%)
  matrix products  18.6 us (8%)
  between operations  13.9 us (6%)
    gather x16, local copies, waits for them, and re-layouts, accumulate(): source = jnp.take(flat_group, index, axis=0)  63.1 us
    all_gather x1, waiting for transfers between devices, body(): group = lax.all_gather(coarse, 'gy', axis=1, tiled=True)  58.1 us
    ppermute x4, starting transfers between devices, extended(): lax.ppermute(tail, axis, [(i, (i + 1) % count) for i in range(ends)])  15.9 us
    sub x23, other arithmetic, complex_flat(): first = table[..., :half] * real_part - table[..., half:] * imag_part  14.4 us
    ppermute x4, starting transfers between devices, extended(): lax.ppermute(head, axis, [((i + 1) % count, i) for i in range(ends)])  10.3 us
    unnamed x47, local copies, waits for them, and re-layouts  7.43 us
    dot_general x16, matrix products, accumulate(): jnp.dot(choose, table, precision=lax.Precision.HIGHEST, preferred_element...  6.53 us
    dot_general x1, matrix products, body(): jnp.dot(incoming.reshape(tile_x * tile_y, 2 * samples), receive_map, pref...  6.53 us
  transfers between devices with their start and end apart: 9, of which 2 were waited for; matrix products, arithmetic and copies ran while one was open for 10% of the time, Pallas kernels for 0%

commit v1 on v0

--- a/solution.py
+++ b/solution.py
@@ -106,7 +106,12 @@
                 child, child_to_parent[2 * half_x + half_y], preferred_element_type=jnp.float32
             )
     coarse = coarse_sum.astype(jnp.bfloat16).reshape(parents_x, parents_y, 2 * parent_samples)
-    group = lax.all_gather(coarse, "gy", axis=1, tiled=True)
+    group = jnp.concatenate(
+        jax.lax.all_to_all(
+            jnp.stack([coarse for _ in range(jax.lax.axis_size("gy"))], axis=0), "gy", 0, 0
+        ),
+        1,
+    )
     flat_group = group.reshape(group.shape[0] * group.shape[1], 2 * parent_samples)
     table = up_translator.reshape(kind_total, 2 * parent_samples)
     coarse_in = translate_group(flat_group, coarse_list, coarse_kind, coarse_count, table)

time: 235 us -> 254 us (1.081)
  the two profiles are of different devices: /device:TPU:8 before, /device:TPU:454 now
where the time goes in v1:
time: 254 us; the launch traced here: 252 us
  local copies, waits for them, and re-layouts  104 us (41%)
  waiting for transfers between devices  64.5 us (25%)
  starting transfers between devices  36 us (14%)
  other arithmetic  28.9 us (11%)
  matrix products  17.8 us (7%)
    gather x16, local copies, waits for them, and re-layouts, accumulate(): source = jnp.take(flat_group, index, axis=0)  63 us
    ppermute x4, waiting for transfers between devices, extended(): lax.ppermute(tail, axis, [(i, (i + 1) % count) for i in range(ends)])  61 us
    ppermute x4, starting transfers between devices, extended(): lax.ppermute(head, axis, [((i + 1) % count, i) for i in range(ends)])  14.3 us
    sub x23, other arithmetic, complex_flat(): first = table[..., :half] * real_part - table[..., half:] * imag_part  14.3 us
    dynamic_slice x16, local copies, waits for them, and re-layouts, accumulate(): index = lists[:, :, slot].reshape(rows_a * rows_b)  11.6 us
    ppermute x4, starting transfers between devices, extended(): lax.ppermute(tail, axis, [(i, (i + 1) % count) for i in range(ends)])  11.5 us
    all_to_all x1, starting transfers between devices, body(): jax.lax.all_to_all(jnp.stack([coarse for _ in range(jax.lax.axis_size('gy...  10.2 us
    unnamed x47, local copies, waits for them, and re-layouts  8.57 us
  transfers between devices with their start and end apart: 9, of which 2 were waited for; matrix products, arithmetic and copies ran while one was open for 9% of the time, Pallas kernels for 0%

profile of v1, /device:TPU:454, one launch (start us, length us, event | category | flops | bytes accessed | tf_op | source)
XLA Modules:
  0.0 252.3 jit_solution(17028456604925404840)
XLA Ops:
  10.0 10.2 %all-to-all-start = ((bf16[16,16,16,512]{3,2,1,0:T(8,128)(2,1)}), bf16[16,16,16,512]{3,2,1,0:T(8,128)(2,1)}, u32[]{:S(2)}, u32[]{:S(2)}) async-start(bf16[16,16,16,512]{3,2,1,0:T(8,128)(2,1)} %stack.18), calls=%async_computation | async-start | bytes 8388608 | tf_op jit(solution)/shard_map/all_to_all | solution.py:110
  36.5 4.0 %collective-permute-start.7 = (bf16[34,1,2,128]{3,2,1,0:T(2,128)(2,1)S(1)}, bf16[34,1,2,128]{3,2,1,0:T(2,128)(2,1)S(1)}, u32[]{:S(2)}, u32[]{:S(2)}) collective-permute-start(bf16[34,1,2,128]{3,2,1,0:T(2,128)(2,1)S(1)} %get-tuple-element.270), channel_id=1, source_target_pairs={{1,0},{2,1},{3,2},{4,3},{5,4},{6,5},{7,6},{8,7},{9,8},{10,9},{11,1... | collective-permute-start | bytes 52232 | tf_op jit(solution)/shard_map/ppermute | solution.py:17
  42.9 4.3 %collective-permute-start.2 = (bf16[36,2,256]{2,1,0:T(2,128)(2,1)S(1)}, bf16[36,2,256]{2,1,0:T(2,128)(2,1)S(1)}, u32[]{:S(2)}, u32[]{:S(2)}) collective-permute-start(bf16[36,2,256]{2,1,0:T(2,128)(2,1)S(1)} %get-tuple-element.256), channel_id=1, source_target_pairs={{0,1},{1,2},{2,3},{3,4},{4,5},{5,6},{6,7},{7,8},{8,9},{9,10},{10,1... | collective-permute-start | bytes 110600 | tf_op jit(solution)/shard_map/ppermute | solution.py:15
  52.6 61.0 %collective-permute-done.6 = bf16[34,1,2,128]{3,2,1,0:T(2,128)(2,1)S(1)} collective-permute-done((bf16[34,1,2,128]{3,2,1,0:T(2,128)(2,1)S(1)}, bf16[34,1,2,128]{3,2,1,0:T(2,128)(2,1)S(1)}, u32[]{:S(2)}, u32[]{:S(2)}) %collective-permute-start.6) | collective-permute-done | bytes 17440 | tf_op jit(solution)/shard_map/ppermute | solution.py:15
  119.2 4.3 %fusion.115 = (bf16[32,32,2,128]{3,2,1,0:T(2,128)(2,1)}, bf16[32,32,2,128]{3,2,1,0:T(2,128)(2,1)}, bf16[32,32,2,128]{3,2,1,0:T(2,128)(2,1)}, bf16[32,32,2,128]{3...) fusion(bf16[34,33,2,128]{3,2,1,0:T(2,128)(2,1)S(1)} %get-tuple-element.268, ...), kind=kLoop, calls=%fused_computation.264 | loop fusion | bytes 6291456 | tf_op jit(solution)/shard_map/slice | solution.py:136
  134.7 4.9 %copy.31 = bf16[16,16,16,512]{3,2,0,1:T(8,128)(2,1)} copy(bf16[16,16,16,512]{3,2,1,0:T(8,128)(2,1)} %all-to-all-done) | data formatting | bytes 8388608 | tf_op jit(solution)/shard_map/all_to_all | solution.py:110
  139.6 92.8 %while.14 = (s32[]{:T(128)}, f32[256,512]{1,0:T(8,128)S(1)}, s32[16,16]{1,0:T(8,128)S(1)}, s32[16,16,16]{1,0,2:T(8,128)}, f32[64,512]{1,0:T(8,128)S(1)}, /*index...) while((s32[]{:T(128)}, f32[256,512]{1,0:T(8,128)S(1)}, ...), condition=%wide.region_1.2_spmd.clone, body=%wide.region_0.1_spmd.clone.sunk | while | flops 101862912 | bytes 4610671 | solution.py:59
  140.5 3.9 %gather_fusion = bf16[256,512]{1,0:T(8,128)(2,1)S(1)} fusion(bf16[4096,512]{1,0:T(8,128)(2,1)} %get-tuple-element.398, s32[1024]{0:T(1024)S(1)} %pad_clamp_fusion.2), kind=kCustom, calls=%fused_computation.clone.clone.1 | custom fusion | bytes 525312 | tf_op jit(solution)/shard_map/while/body/eval_jaxpr/jit(_take)/gather | solution.py:47
  146.3 3.9 %gather_fusion = bf16[256,512]{1,0:T(8,128)(2,1)S(1)} fusion(bf16[4096,512]{1,0:T(8,128)(2,1)} %get-tuple-element.398, s32[1024]{0:T(1024)S(1)} %pad_clamp_fusion.2), kind=kCustom, calls=%fused_computation.clone.clone.1 | custom fusion | bytes 525312 | tf_op jit(solution)/shard_map/while/body/eval_jaxpr/jit(_take)/gather | solution.py:47
  152.1 3.9 %gather_fusion = bf16[256,512]{1,0:T(8,128)(2,1)S(1)} fusion(bf16[4096,512]{1,0:T(8,128)(2,1)} %get-tuple-element.398, s32[1024]{0:T(1024)S(1)} %pad_clamp_fusion.2), kind=kCustom, calls=%fused_computation.clone.clone.1 | custom fusion | bytes 525312 | tf_op jit(solution)/shard_map/while/body/eval_jaxpr/jit(_take)/gather | solution.py:47
  157.9 3.9 %gather_fusion = bf16[256,512]{1,0:T(8,128)(2,1)S(1)} fusion(bf16[4096,512]{1,0:T(8,128)(2,1)} %get-tuple-element.398, s32[1024]{0:T(1024)S(1)} %pad_clamp_fusion.2), kind=kCustom, calls=%fused_computation.clone.clone.1 | custom fusion | bytes 525312 | tf_op jit(solution)/shard_map/while/body/eval_jaxpr/jit(_take)/gather | solution.py:47
  163.6 3.9 %gather_fusion = bf16[256,512]{1,0:T(8,128)(2,1)S(1)} fusion(bf16[4096,512]{1,0:T(8,128)(2,1)} %get-tuple-element.398, s32[1024]{0:T(1024)S(1)} %pad_clamp_fusion.2), kind=kCustom, calls=%fused_computation.clone.clone.1 | custom fusion | bytes 525312 | tf_op jit(solution)/shard_map/while/body/eval_jaxpr/jit(_take)/gather | solution.py:47
  169.4 3.9 %gather_fusion = bf16[256,512]{1,0:T(8,128)(2,1)S(1)} fusion(bf16[4096,512]{1,0:T(8,128)(2,1)} %get-tuple-element.398, s32[1024]{0:T(1024)S(1)} %pad_clamp_fusion.2), kind=kCustom, calls=%fused_computation.clone.clone.1 | custom fusion | bytes 525312 | tf_op jit(solution)/shard_map/while/body/eval_jaxpr/jit(_take)/gather | solution.py:47
  175.2 3.9 %gather_fusion = bf16[256,512]{1,0:T(8,128)(2,1)S(1)} fusion(bf16[4096,512]{1,0:T(8,128)(2,1)} %get-tuple-element.398, s32[1024]{0:T(1024)S(1)} %pad_clamp_fusion.2), kind=kCustom, calls=%fused_computation.clone.clone.1 | custom fusion | bytes 525312 | tf_op jit(solution)/shard_map/while/body/eval_jaxpr/jit(_take)/gather | solution.py:47
  181.0 3.9 %gather_fusion = bf16[256,512]{1,0:T(8,128)(2,1)S(1)} fusion(bf16[4096,512]{1,0:T(8,128)(2,1)} %get-tuple-element.398, s32[1024]{0:T(1024)S(1)} %pad_clamp_fusion.2), kind=kCustom, calls=%fused_computation.clone.clone.1 | custom fusion | bytes 525312 | tf_op jit(solution)/shard_map/while/body/eval_jaxpr/jit(_take)/gather | solution.py:47
  186.8 3.9 %gather_fusion = bf16[256,512]{1,0:T(8,128)(2,1)S(1)} fusion(bf16[4096,512]{1,0:T(8,128)(2,1)} %get-tuple-element.398, s32[1024]{0:T(1024)S(1)} %pad_clamp_fusion.2), kind=kCustom, calls=%fused_computation.clone.clone.1 | custom fusion | bytes 525312 | tf_op jit(solution)/shard_map/while/body/eval_jaxpr/jit(_take)/gather | solution.py:47
  192.6 3.9 %gather_fusion = bf16[256,512]{1,0:T(8,128)(2,1)S(1)} fusion(bf16[4096,512]{1,0:T(8,128)(2,1)} %get-tuple-element.398, s32[1024]{0:T(1024)S(1)} %pad_clamp_fusion.2), kind=kCustom, calls=%fused_computation.clone.clone.1 | custom fusion | bytes 525312 | tf_op jit(solution)/shard_map/while/body/eval_jaxpr/jit(_take)/gather | solution.py:47
  198.4 3.9 %gather_fusion = bf16[256,512]{1,0:T(8,128)(2,1)S(1)} fusion(bf16[4096,512]{1,0:T(8,128)(2,1)} %get-tuple-element.398, s32[1024]{0:T(1024)S(1)} %pad_clamp_fusion.2), kind=kCustom, calls=%fused_computation.clone.clone.1 | custom fusion | bytes 525312 | tf_op jit(solution)/shard_map/while/body/eval_jaxpr/jit(_take)/gather | solution.py:47
  204.2 3.9 %gather_fusion = bf16[256,512]{1,0:T(8,128)(2,1)S(1)} fusion(bf16[4096,512]{1,0:T(8,128)(2,1)} %get-tuple-element.398, s32[1024]{0:T(1024)S(1)} %pad_clamp_fusion.2), kind=kCustom, calls=%fused_computation.clone.clone.1 | custom fusion | bytes 525312 | tf_op jit(solution)/shard_map/while/body/eval_jaxpr/jit(_take)/gather | solution.py:47
  210.0 3.9 %gather_fusion = bf16[256,512]{1,0:T(8,128)(2,1)S(1)} fusion(bf16[4096,512]{1,0:T(8,128)(2,1)} %get-tuple-element.398, s32[1024]{0:T(1024)S(1)} %pad_clamp_fusion.2), kind=kCustom, calls=%fused_computation.clone.clone.1 | custom fusion | bytes 525312 | tf_op jit(solution)/shard_map/while/body/eval_jaxpr/jit(_take)/gather | solution.py:47
  215.8 3.9 %gather_fusion = bf16[256,512]{1,0:T(8,128)(2,1)S(1)} fusion(bf16[4096,512]{1,0:T(8,128)(2,1)} %get-tuple-element.398, s32[1024]{0:T(1024)S(1)} %pad_clamp_fusion.2), kind=kCustom, calls=%fused_computation.clone.clone.1 | custom fusion | bytes 525312 | tf_op jit(solution)/shard_map/while/body/eval_jaxpr/jit(_take)/gather | solution.py:47
  221.6 3.9 %gather_fusion = bf16[256,512]{1,0:T(8,128)(2,1)S(1)} fusion(bf16[4096,512]{1,0:T(8,128)(2,1)} %get-tuple-element.398, s32[1024]{0:T(1024)S(1)} %pad_clamp_fusion.2), kind=kCustom, calls=%fused_computation.clone.clone.1 | custom fusion | bytes 525312 | tf_op jit(solution)/shard_map/while/body/eval_jaxpr/jit(_take)/gather | solution.py:47
  227.4 3.9 %gather_fusion = bf16[256,512]{1,0:T(8,128)(2,1)S(1)} fusion(bf16[4096,512]{1,0:T(8,128)(2,1)} %get-tuple-element.398, s32[1024]{0:T(1024)S(1)} %pad_clamp_fusion.2), kind=kCustom, calls=%fused_computation.clone.clone.1 | custom fusion | bytes 525312 | tf_op jit(solution)/shard_map/while/body/eval_jaxpr/jit(_take)/gather | solution.py:47
  235.3 6.5 %fusion.74 = f32[1024,256]{1,0:T(8,128)S(1)} fusion(bf16[256,256]{1,0:T(8,128)(2,1)S(1)} %copy-done.15, f32[1024,256]{1,0:T(8,128)S(1)} %reshape.260, f32[1024,128]{1,0:T(8,128)} %bitcast.278, f32[1024,128]{1,0:T(8,128)} %bitcast.279, f32[1024,128]{1,0:T(8,128)} %bitcast.280, f32[1024,128]{1,0:T(8,128)} %bitcast.281, f32[1024,128]{1,0:T(8,128)} %bitcast.291, ...), kind=kOutput, calls=%fused_computation.182 | convolution fusion | flops 142868480 | bytes 19005440 | tf_op jit(solution)/shard_map/dot_general | solution.py:129
  (316 shorter events, 92.8 us)
Async XLA Ops:
  0.0 3.7 %copy-start = (bf16[256,256]{1,0:T(8,128)(2,1)S(1)}, bf16[256,256]{1,0:T(8,128)(2,1)}, u32[]{:S(2)}) copy-start(bf16[256,256]{1,0:T(8,128)(2,1)} %param.16) | copy-start | bytes 393220
  5.3 1.2 copy-start.13
  10.0 21.4 %copy-start.19 = (f32[16,2,128]{2,1,0:T(2,128)S(1)}, f32[16,2,128]{2,1,0:T(2,128)}, u32[]{:S(2)}) copy-start(f32[16,2,128]{2,1,0:T(2,128)} %param.18) | copy-start | bytes 49156
  10.0 21.5 %copy-start.16 = (f32[64,2,256]{2,1,0:T(2,128)S(1)}, f32[64,2,256]{2,1,0:T(2,128)}, u32[]{:S(2)}) copy-start(f32[64,2,256]{2,1,0:T(2,128)} %param.23) | copy-start | bytes 393220
  10.0 21.5 %copy-start.17 = (s32[16,16,16]{2,1,0:T(8,128)S(1)}, s32[16,16,16]{2,1,0:T(8,128)}, u32[]{:S(2)}) copy-start(s32[16,16,16]{2,1,0:T(8,128)} %param.21) | copy-start | bytes 49156
  10.0 22.3 %copy-start.18 = (s32[16,16,16]{2,1,0:T(8,128)S(1)}, s32[16,16,16]{2,1,0:T(8,128)}, u32[]{:S(2)}) copy-start(s32[16,16,16]{2,1,0:T(8,128)} %param.20) | copy-start | bytes 49156
  10.0 124.6 %all-to-all-start = ((bf16[16,16,16,512]{3,2,1,0:T(8,128)(2,1)}), bf16[16,16,16,512]{3,2,1,0:T(8,128)(2,1)}, u32[]{:S(2)}, u32[]{:S(2)}) async-start(bf16[16,16,16,512]{3,2,1,0:T(8,128)(2,1)} %stack.18), calls=%async_computation | async-start | bytes 8388608 | tf_op jit(solution)/shard_map/all_to_all | solution.py:110
  20.3 22.6 %collective-permute-start = (bf16[2,32,256]{2,1,0:T(8,128)(2,1)S(1)}, bf16[2,32,256]{2,1,0:T(8,128)(2,1)S(1)}, u32[]{:S(2)}, u32[]{:S(2)}) collective-permute-start(bf16[2,32,256]{2,1,0:T(8,128)(2,1)S(1)} %bitcast.306), channel_id=1, source_target_pairs={{0,16},{16,32},{32,48},{48,64},{64,80},{80,96},{96,112},{112,128},... | collective-permute-start | bytes 98312 | tf_op jit(solution)/shard_map/ppermute | solution.py:15
  22.2 20.7 %collective-permute-start.1 = (bf16[2,32,256]{2,1,0:T(8,128)(2,1)S(1)}, bf16[2,32,256]{2,1,0:T(8,128)(2,1)S(1)}, u32[]{:S(2)}, u32[]{:S(2)}) collective-permute-start(bf16[2,32,256]{2,1,0:T(8,128)(2,1)S(1)} %bitcast.305), channel_id=1, source_target_pairs={{16,0},{32,16},{48,32},{64,48},{80,64},{96,80},{112,96},{128,112},... | collective-permute-start | bytes 98312 | tf_op jit(solution)/shard_map/ppermute | solution.py:17
  25.9 7.2 %collective-permute-start.4 = (bf16[1,32,2,128]{3,2,1,0:T(2,128)(2,1)S(1)}, bf16[1,32,2,128]{3,2,1,0:T(2,128)(2,1)S(1)}, u32[]{:S(2)}, u32[]{:S(2)}) collective-permute-start(bf16[1,32,2,128]{3,2,1,0:T(2,128)(2,1)S(1)} %get-tuple-element.274), channel_id=1, source_target_pairs={{0,16},{16,32},{32,48},{48,64},{64,80},{80,96},{96,112},{112,128},... | collective-permute-start | bytes 49160 | tf_op jit(solution)/shard_map/ppermute | solution.py:15
  27.8 5.3 %collective-permute-start.5 = (bf16[1,32,2,128]{3,2,1,0:T(2,128)(2,1)S(1)}, bf16[1,32,2,128]{3,2,1,0:T(2,128)(2,1)S(1)}, u32[]{:S(2)}, u32[]{:S(2)}) collective-permute-start(bf16[1,32,2,128]{3,2,1,0:T(2,128)(2,1)S(1)} %get-tuple-element.275), channel_id=1, source_target_pairs={{16,0},{32,16},{48,32},{64,48},{80,64},{96,80},{112,96},{128,112},... | collective-permute-start | bytes 49160 | tf_op jit(solution)/shard_map/ppermute | solution.py:17
  33.2 80.4 %collective-permute-start.6 = (bf16[34,1,2,128]{3,2,1,0:T(2,128)(2,1)S(1)}, bf16[34,1,2,128]{3,2,1,0:T(2,128)(2,1)S(1)}, u32[]{:S(2)}, u32[]{:S(2)}) collective-permute-start(bf16[34,1,2,128]{3,2,1,0:T(2,128)(2,1)S(1)} %get-tuple-element.271), channel_id=1, source_target_pairs={{0,1},{1,2},{2,3},{3,4},{4,5},{5,6},{6,7},{7,8},{8,9},{9,10},{10,1... | collective-permute-start | bytes 52232 | tf_op jit(solution)/shard_map/ppermute | solution.py:15
  36.5 80.5 %collective-permute-start.7 = (bf16[34,1,2,128]{3,2,1,0:T(2,128)(2,1)S(1)}, bf16[34,1,2,128]{3,2,1,0:T(2,128)(2,1)S(1)}, u32[]{:S(2)}, u32[]{:S(2)}) collective-permute-start(bf16[34,1,2,128]{3,2,1,0:T(2,128)(2,1)S(1)} %get-tuple-element.270), channel_id=1, source_target_pairs={{1,0},{2,1},{3,2},{4,3},{5,4},{6,5},{7,6},{8,7},{9,8},{10,9},{11,1... | collective-permute-start | bytes 52232 | tf_op jit(solution)/shard_map/ppermute | solution.py:17
  42.9 80.6 %collective-permute-start.2 = (bf16[36,2,256]{2,1,0:T(2,128)(2,1)S(1)}, bf16[36,2,256]{2,1,0:T(2,128)(2,1)S(1)}, u32[]{:S(2)}, u32[]{:S(2)}) collective-permute-start(bf16[36,2,256]{2,1,0:T(2,128)(2,1)S(1)} %get-tuple-element.256), channel_id=1, source_target_pairs={{0,1},{1,2},{2,3},{3,4},{4,5},{5,6},{6,7},{7,8},{8,9},{9,10},{10,1... | collective-permute-start | bytes 110600 | tf_op jit(solution)/shard_map/ppermute | solution.py:15
  47.2 76.3 %collective-permute-start.3 = (bf16[36,2,256]{2,1,0:T(2,128)(2,1)S(1)}, bf16[36,2,256]{2,1,0:T(2,128)(2,1)S(1)}, u32[]{:S(2)}, u32[]{:S(2)}) collective-permute-start(bf16[36,2,256]{2,1,0:T(2,128)(2,1)S(1)} %get-tuple-element.257), channel_id=1, source_target_pairs={{1,0},{2,1},{3,2},{4,3},{5,4},{6,5},{7,6},{8,7},{9,8},{10,9},{11,1... | collective-permute-start | bytes 110600 | tf_op jit(solution)/shard_map/ppermute | solution.py:17
  134.7 4.9 %copy-start.14 = (s32[16,16]{1,0:T(8,128)S(1)}, s32[16,16]{1,0:T(8,128)}, u32[]{:S(2)}) copy-start(s32[16,16]{1,0:T(8,128)} %param.22) | copy-start | bytes 3076
  139.6 92.9 %copy-start.12 = (bf16[4,512,256]{2,1,0:T(8,128)(2,1)S(1)}, bf16[4,512,256]{2,1,0:T(8,128)(2,1)}, u32[]{:S(2)}) copy-start(bf16[4,512,256]{2,1,0:T(8,128)(2,1)} %param.24) | copy-start | bytes 3145732
  235.3 6.5 %copy-start.10 = (bf16[32,32,2,128]{3,2,1,0:T(2,128)(2,1)S(1)}, bf16[32,32,2,128]{3,2,1,0:T(2,128)(2,1)}, u32[]{:S(2)}) copy-start(bf16[32,32,2,128]{3,2,1,0:T(2,128)(2,1)} %get-tuple-element.316) | copy-start | bytes 1572868
  235.3 6.5 %copy-start.11 = (bf16[9,256,256]{2,1,0:T(8,128)(2,1)S(1)}, bf16[9,256,256]{2,1,0:T(8,128)(2,1)}, u32[]{:S(2)}) copy-start(bf16[9,256,256]{2,1,0:T(8,128)(2,1)} %param.17) | copy-start | bytes 3538948
  241.9 1.0 copy-start.4
  242.9 1.0 copy-start.9
  245.3 1.0 copy-start.7
  249.7 1.0 copy-start.2
  250.3 2.0 copy-start.1
  (5 other events, 5.1 us)
